TPU v7x, 32 devices: a whole 2x2x4 slice. The times are simulated.
32 devices in a mesh: row: 4 (over y, x), col: 8 (over z, core).
Axes of the slice: x: 2, y: 2, z: 4, core: 2. Of those that a mesh axis runs over, the one named last changes fastest.
Arguments:
- tokens: bfloat16 [512, 5120], P('row'), may hold values from -6 to 6
- expert_ids: int32 [512], replicated, may hold values from 0 to 7
- modality: int32 [512], replicated, may hold values from 0 to 1
- tile_counts: int32 [2, 8], replicated, may hold values from 1 to 4, as said below
- router: bfloat16 [5120, 8], P(None, 'col'), may hold values from -0.15625 to 0.15625
- w_gate: bfloat16 [8, 5120, 4096], P('col', None, 'row'), may hold values from -0.078125 to 0.078125
- w_up: bfloat16 [8, 5120, 4096], P('col', None, 'row'), may hold values from -0.078125 to 0.078125
- w_down: bfloat16 [8, 4096, 5120], P('col', 'row'), may hold values from -0.09375 to 0.09375
- shared_gate: bfloat16 [5120, 8192], P('row', 'col'), may hold values from -0.078125 to 0.078125
- shared_up: bfloat16 [5120, 8192], P('row', 'col'), may hold values from -0.078125 to 0.078125
- shared_down: bfloat16 [8192, 5120], P('col', 'row'), may hold values from -0.0625 to 0.0625
Outputs:
- mixed: bfloat16 [512, 5120], P('col', 'row')
Inputs may be any that keep to these rules, and one draw needn't show every extreme that they name: `tile_counts`: in every draw some expert's text segment has 4 tiles and at least 32 text tokens, and some expert's image segment has 4 tiles and at least 32 image tokens.
All inputs are finite; a program needn't handle non-finite values.
Results may differ from a plain program's by a relative error of at most 0.0052.
Values may be sent and summed in bfloat16 or wider, within the bound.
No kernel may reach another device: no remote copies, remote signals or barrier semaphores. Data moves between devices by JAX's collectives and lax.ppermute only.
A program may use at most 128 MiB of HBM per device.

v0:
```python
import jax
import jax.numpy as jnp
from jax import lax
from jax.sharding import PartitionSpec as P

TILE = 8
MAXT = 4


def slot_places(expert_ids, modality, tile_counts, expert):
    capacity = MAXT * TILE
    places = jnp.full(expert_ids.shape, -1, jnp.int32)
    for kind in range(2):
        member = ((expert_ids == expert) & (modality == kind)).astype(jnp.int32)
        rank = jnp.cumsum(member, dtype=jnp.int32) - 1
        limit = tile_counts[kind, expert] * TILE
        keep = (member == 1) & (rank < limit)
        places = jnp.where(keep, kind * capacity + rank, places)
    return places


def slot_table(places):
    slots = lax.broadcasted_iota(jnp.int32, (2 * MAXT * TILE, places.shape[0]), 0)
    return (slots == places[None, :]).astype(jnp.bfloat16)


def place_rows(places, values):
    index = jnp.maximum(places, 0)
    rows = jnp.take(values, index, axis=0)
    return jnp.where((places >= 0)[:, None], rows, jnp.zeros_like(rows))


def per_device(
    tokens,
    expert_ids,
    modality,
    tile_counts,
    router,
    w_gate,
    w_up,
    w_down,
    shared_gate,
    shared_up,
    shared_down,
):
    whole = lax.all_gather(tokens, "row", axis=0, tiled=True)
    expert = lax.axis_index("col")
    places = slot_places(expert_ids, modality, tile_counts, expert)
    table = slot_table(places)
    taken = jnp.dot(table, whole, preferred_element_type=jnp.float32).astype(jnp.bfloat16)
    score = jax.nn.sigmoid(jnp.dot(taken, router, preferred_element_type=jnp.float32))
    scaled = (taken.astype(jnp.float32) * score).astype(jnp.bfloat16)
    gate = jnp.dot(scaled, w_gate[0], preferred_element_type=jnp.float32)
    upper = jnp.dot(scaled, w_up[0], preferred_element_type=jnp.float32)
    hidden = (jax.nn.silu(gate) * upper).astype(jnp.bfloat16)
    result = jnp.dot(hidden, w_down[0], preferred_element_type=jnp.float32)
    width_row = shared_down.shape[1]
    feature_start = lax.axis_index("row") * width_row
    local_rows = lax.dynamic_slice_in_dim(whole, feature_start, width_row, 1)
    gate_part = jnp.dot(local_rows, shared_gate, preferred_element_type=jnp.float32)
    upper_part = jnp.dot(local_rows, shared_up, preferred_element_type=jnp.float32)
    shared_gate_sum, shared_up_sum = lax.psum((gate_part, upper_part), "row")
    shared_hidden = (jax.nn.silu(shared_gate_sum) * shared_up_sum).astype(jnp.bfloat16)
    shared_part = jnp.dot(shared_hidden, shared_down, preferred_element_type=jnp.float32)
    slot_total = lax.psum_scatter(result, "row", scatter_dimension=1, tiled=True)
    combined = place_rows(places, slot_total) + shared_part
    total = lax.psum_scatter(combined, "col", scatter_dimension=0, tiled=True)
    return total.astype(jnp.bfloat16)


def solution(mesh):
    in_specs = (
        P("row", None),
        P(),
        P(),
        P(),
        P(None, "col"),
        P("col", None, "row"),
        P("col", None, "row"),
        P("col", "row", None),
        P("row", "col"),
        P("row", "col"),
        P("col", "row"),
    )
    out_specs = P("col", "row")
    return jax.shard_map(
        per_device, mesh=mesh, in_specs=in_specs, out_specs=out_specs, check_vma=False
    )
```

profile of v0, /device:TPU:0, one launch (start us, length us, event | category | flops | bytes accessed | tf_op | source)
XLA Modules:
  0.0 284.3 jit_solution(9219536786317185767)
XLA Ops:
  6.5 0.0 copy-start
  6.5 0.7 all-gather.2.cloned.1.call-update
  7.3 0.0 reduce-scatter.3.cloned.1.call-start
  7.3 1.4 constant_dynamic-slice_fusion.1
  10.0 0.7 convert_bitcast_fusion
  10.7 0.3 reduce-window.24
  11.0 0.1 slice.16
  11.1 0.7 convert_bitcast_fusion.1
  11.8 0.3 reduce-window.16
  12.1 0.1 slice.14
  12.2 0.1 slice_reduce_fusion
  12.3 0.1 broadcast_compare_fusion.1
  12.4 60.8 %all-gather.2.cloned.1.call-done = bf16[512,5120]{1,0:T(8,128)(2,1)} async-done(((bf16[128,5120]{1,0:T(8,128)(2,1)}), bf16[512,5120]{1,0:T(8,128)(2,1)}) %all-gather.2.cloned.1.call-update) | async-done | bytes 5242896 | tf_op jit(solution)/shard_map/all_gather | solution.py:46
  73.2 3.5 %convolution_convert_fusion = bf16[64,5120]{1,0:T(8,128)(2,1)S(1)} fusion(bf16[512,5120]{1,0:T(8,128)(2,1)} %all-gather.2.cloned.1.call-done, s32[512]{0:T(512)S(1)} %get-tuple-element.8), kind=kOutput, calls=%fused_computation.7 | convolution fusion | flops 335904768 | bytes 5900288 | tf_op jit(solution)/shard_map/dot_general | solution.py:50
  76.8 0.0 copy-done.2
  76.8 0.3 fusion.19
  77.0 6.0 %fusion.4 = f32[64,1024]{1,0:T(8,128)S(1)} fusion(bf16[1,5120,1024]{2,1,0:T(8,128)(2,1)} %param.16, bf16[64,5120]{1,0:T(8,128)(2,1)S(1)} %convolution_convert_fusion, f32[64]{0:T(128)S(1)} %fusion.19), kind=kOutput, calls=%fused_computation.5 | convolution fusion | flops 672071680 | bytes 11403520 | tf_op jit(solution)/shard_map/dot_general | solution.py:53
  83.0 11.9 %fusion = f32[64,5120]{1,0:T(8,128)} fusion(bf16[1,1024,5120]{2,1,0:T(8,128)(2,1)} %param.18, bf16[1,5120,1024]{2,1,0:T(8,128)(2,1)} %param.17, bf16[64,5120]{1,0:T(8,128)(2,1)S(1)} %convolution_convert_fusion, f32[64]{0:T(128)S(1)} %fusion.19, f32[64,1024]{1,0:T(8,128)S(1)} %fusion.4), kind=kOutput, calls=%fused_computation.1 | convolution fusion | flops 1343553536 | bytes 23200000 | tf_op jit(solution)/shard_map/dot_general | solution.py:56
  94.9 0.0 reduce-scatter.3.cloned.1.call-update
  94.9 0.0 all-reduce.3.cloned.1.call-start
  95.0 0.0 copy-start.1
  95.0 5.2 %fusion.9 = f32[512,1024]{1,0:T(8,128)} fusion(bf16[1280,1024]{1,0:T(8,128)(2,1)} %param.20, bf16[512,5120]{1,0:T(8,128)(2,1)} %all-gather.2.cloned.1.call-done, s32[]{:T(128)S(6)} %select_n.29), kind=kOutput, calls=%fused_computation.12 | convolution fusion | flops 1342177280 | bytes 6029316 | tf_op jit(solution)/shard_map/dot_general | solution.py:61
  100.2 4.2 %fusion.11 = f32[512,1024]{1,0:T(8,128)} fusion(bf16[1280,1024]{1,0:T(8,128)(2,1)S(1)} %copy-done.1, bf16[512,5120]{1,0:T(8,128)(2,1)} %all-gather.2.cloned.1.call-done, s32[]{:T(128)S(6)} %select_n.29), kind=kOutput, calls=%fused_computation.14 | convolution fusion | flops 1342177280 | bytes 6029316 | tf_op jit(solution)/shard_map/dot_general | solution.py:60
  104.4 0.0 all-reduce.3.cloned.1.call-update
  104.5 0.0 reduce-scatter.5.cloned.1.call-start
  104.6 20.0 %reduce-scatter.3.cloned.1.call-done = f32[64,1280]{1,0:T(8,128)} async-done(((f32[64,5120]{1,0:T(8,128)}), f32[64,1280]{1,0:T(8,128)}) %reduce-scatter.3.cloned.1.call-update) | async-done | bytes 327696 | tf_op jit(solution)/shard_map/reduce_scatter | solution.py:65
  124.6 5.0 %gather_fusion = f32[512,1280]{1,0:T(8,128)} fusion(f32[64,1280]{1,0:T(8,128)} %reduce-scatter.3.cloned.1.call-done, s32[1024]{0:T(1024)S(1)} %pad_clamp_fusion), kind=kCustom, calls=%fused_computation | custom fusion | bytes 5244928 | tf_op jit(solution)/shard_map/jit(_take)/gather | solution.py:29
  129.6 102.1 %all-reduce.3.cloned.1.call-done = (f32[512,1024]{1,0:T(8,128)}, f32[512,1024]{1,0:T(8,128)}) async-done(((f32[512,1024]{1,0:T(8,128)}, f32[512,1024]{1,0:T(8,128)}), (f32[512,1024]{1,0:T(8,128)}, f32[512,1024]{1,0:T(8,128)})) %all-reduce.3.cloned.1.call-update) | async-done | bytes 4194320 | tf_op jit(solution)/shard_map/psum | solution.py:62
  231.7 6.4 %convolution_add_fusion = f32[512,1280]{1,0:T(8,128)} fusion(bf16[1024,1280]{1,0:T(8,128)(2,1)S(1)} %copy-done, f32[512,1280]{1,0:T(8,128)} %gather_fusion, pred[512]{0:T(512)(128)(4,1)S(1)} %broadcast_compare_fusion, pred[512]{0:T(512)(128)(4,1)S(1)} %get-tuple-element.7, f32[512,1024]{1,0:T(8,128)} %get-tuple-element.5, f32[512,1024]{1,0:T(8,128)} %get-tuple-element.6), kind=kOutput, calls=%fused_computation.8 | convolution fusion | flops 1347289088 | bytes 12059648 | tf_op jit(solution)/shard_map/dot_general | solution.py:64
  238.1 0.0 reduce-scatter.5.cloned.1.call-update
  238.2 38.0 %reduce-scatter.5.cloned.1.call-done = f32[64,1280]{1,0:T(8,128)} async-done(((f32[512,1280]{1,0:T(8,128)}), f32[64,1280]{1,0:T(8,128)}) %reduce-scatter.5.cloned.1.call-update) | async-done | bytes 327696 | tf_op jit(solution)/shard_map/reduce_scatter | solution.py:67
  276.1 1.7 convert_element_type.32
  (9 shorter events, 0.1 us)
Async XLA Ops:
  6.5 225.2 %copy-start = (bf16[1024,1280]{1,0:T(8,128)(2,1)S(1)}, bf16[1024,1280]{1,0:T(8,128)(2,1)}, u32[]{:S(2)}) copy-start(bf16[1024,1280]{1,0:T(8,128)(2,1)} %param.21) | copy-start | bytes 7864324
  6.5 66.7 %all-gather.2.cloned.1.call-start = ((), (), s32[]{:S(2)}) async-start(), calls=%async_computation.2 | async-start | bytes 6553600 | tf_op jit(solution)/shard_map/all_gather | solution.py:46
  7.3 117.3 %reduce-scatter.3.cloned.1.call-start = ((), (), s32[]{:S(2)}) async-start(), calls=%async_computation.3 | async-start | bytes 1638400 | tf_op jit(solution)/shard_map/reduce_scatter | solution.py:65
  73.2 3.5 %copy-start.2 = (bf16[5120,1]{0,1:T(2,128)(2,1)S(1)}, bf16[5120,1]{0,1:T(2,128)(2,1)}, u32[]{:S(2)}) copy-start(bf16[5120,1]{0,1:T(2,128)(2,1)} %param.15) | copy-start | bytes 30724
  94.9 136.8 %all-reduce.3.cloned.1.call-start = ((), (), s32[]{:S(2)}) async-start(), calls=%async_computation.5 | async-start | bytes 8388608 | tf_op jit(solution)/shard_map/psum | solution.py:62
  95.0 5.2 %copy-start.1 = (bf16[1280,1024]{1,0:T(8,128)(2,1)S(1)}, bf16[1280,1024]{1,0:T(8,128)(2,1)}, u32[]{:S(2)}) copy-start(bf16[1280,1024]{1,0:T(8,128)(2,1)} %param.19) | copy-start | bytes 7864324
  104.5 171.7 %reduce-scatter.5.cloned.1.call-start = ((), (), s32[]{:S(2)}) async-start(), calls=%async_computation.4 | async-start | bytes 2949120 | tf_op jit(solution)/shard_map/reduce_scatter | solution.py:67
Sparse Core Ops, SparseCore 0:
  9.2 64.0 all-gather.1
  95.0 29.4 reduce-scatter.2
  128.1 103.5 all-reduce.2
  238.3 37.8 reduce-scatter.4
where the time goes:
time: 285 us; the launch traced here: 284 us
  waiting for transfers between devices  222 us (78%)
  matrix products  37.5 us (13%)
  between operations  14.5 us (5%)
  local copies, waits for them, and re-layouts  6.72 us (2%)
  other arithmetic  3.83 us (1%)
    psum x1, waiting for transfers between devices, per_device(): shared_gate_sum, shared_up_sum = lax.psum((gate_part, upper_part), 'row')  102 us
    all_gather x1, waiting for transfers between devices, per_device(): whole = lax.all_gather(tokens, 'row', axis=0, tiled=True)  60.8 us
    reduce_scatter x1, waiting for transfers between devices, per_device(): total = lax.psum_scatter(combined, 'col', scatter_dimension=0, tiled=True)  38 us
    reduce_scatter x1, waiting for transfers between devices, per_device(): lax.psum_scatter(result, 'row', scatter_dimension=1, tiled=True)  20 us
    dot_general x1, matrix products, per_device(): result = jnp.dot(hidden, w_down[0], preferred_element_type=jnp.float32)  11.9 us
    dot_general x1, matrix products, per_device(): jnp.dot(shared_hidden, shared_down, preferred_element_type=jnp.float32)  6.44 us
    dot_general x1, matrix products, per_device(): gate = jnp.dot(scaled, w_gate[0], preferred_element_type=jnp.float32)  5.99 us
  transfers between devices with their start and end apart: 4, of which 4 were waited for; matrix products, arithmetic and copies ran while one was open for 6% of the time, Pallas kernels for 0%

commit v1 on v0

--- a/solution.py
+++ b/solution.py
@@ -1,3 +1,4 @@
+import functools
 import jax
 import jax.numpy as jnp
 from jax import lax
@@ -5,6 +6,25 @@
 
 TILE = 8
 MAXT = 4
+
+
+def assign_patches(my_data, axis_key):
+    block_out = lax.psum(1, axis_name=axis_key)
+    inter = lax.axis_index(axis_key)
+    raw_out, met_up, part_next = (block_out, inter, my_data.shape[0])
+    block_last, t1 = (my_data, 1)
+    while t1 < raw_out:
+        plain = lax.ppermute(
+            block_last,
+            axis_name=axis_key,
+            perm=[(pp, (pp - t1) % raw_out) for pp in range(raw_out)],
+        )
+        block_last = jnp.concatenate([block_last, plain], axis=0)
+        t1 = 2 * t1
+    return jnp.roll(block_last, met_up * part_next, axis=0)
+
+
+apply_the_panel = functools.partial(assign_patches, axis_key="row")
 
 
 def slot_places(expert_ids, modality, tile_counts, expert):
@@ -43,7 +63,7 @@
     shared_up,
     shared_down,
 ):
-    whole = lax.all_gather(tokens, "row", axis=0, tiled=True)
+    whole = apply_the_panel(tokens)
     expert = lax.axis_index("col")
     places = slot_places(expert_ids, modality, tile_counts, expert)
     table = slot_table(places)

time: 285 us -> 316 us (1.11)
  waiting for transfers between devices: 222 us -> 242 us
  local copies, waits for them, and re-layouts: 6.72 us -> 15.9 us
  matrix products: 37.5 us -> 31.2 us
  starting transfers between devices: 0.12 us -> 5.72 us
    ppermute x0 -> x2, waiting for transfers between devices: none -> 80.2 us  [assign_patches(): lax.ppermute(block_last, axis_name=axis_key, perm=[(pp, (pp - t1) % raw_o...]
    all_gather x1 -> x0, waiting for transfers between devices: 60.8 us -> none  [per_device(): whole = lax.all_gather(tokens, 'row', axis=0, tiled=True)]
    unnamed x6 -> x31, local copies, waits for them, and re-layouts: 0.01 us -> 7.88 us
    ppermute x0 -> x2, starting transfers between devices: none -> 5.42 us  [assign_patches(): lax.ppermute(block_last, axis_name=axis_key, perm=[(pp, (pp - t1) % raw_o...]
    dot_general x1, matrix products: 5.99 us -> 2.02 us  [per_device(): gate = jnp.dot(scaled, w_gate[0], preferred_element_type=jnp.float32)]
    concatenate x0 -> x1, other arithmetic: none -> 3.48 us  [assign_patches(): block_last = jnp.concatenate([block_last, plain], axis=0)]
  transfers between devices with their start and end apart: 4 -> 5, of which waited for: 4 -> 5; matrix products, arithmetic and copies ran while one was open for 6% -> 6% of each run, Pallas kernels for 0% -> 0%
where the time goes in v1:
time: 316 us
  waiting for transfers between devices  242 us (77%)
  matrix products  31.2 us (10%)
  local copies, waits for them, and re-layouts  15.9 us (5%)
  between operations  14.7 us (5%)
  other arithmetic  5.93 us (2%)
  starting transfers between devices  5.72 us (2%)
    psum x1, waiting for transfers between devices, per_device(): shared_gate_sum, shared_up_sum = lax.psum((gate_part, upper_part), 'row')  102 us
    ppermute x2, waiting for transfers between devices, assign_patches(): lax.ppermute(block_last, axis_name=axis_key, perm=[(pp, (pp - t1) % raw_o...  80.2 us
    reduce_scatter x1, waiting for transfers between devices, per_device(): total = lax.psum_scatter(combined, 'col', scatter_dimension=0, tiled=True)  38 us
    reduce_scatter x1, waiting for transfers between devices, per_device(): lax.psum_scatter(result, 'row', scatter_dimension=1, tiled=True)  21.8 us
    dot_general x1, matrix products, per_device(): result = jnp.dot(hidden, w_down[0], preferred_element_type=jnp.float32)  11.9 us
    unnamed x31, local copies, waits for them, and re-layouts  7.88 us
    dot_general x1, matrix products, per_device(): jnp.dot(shared_hidden, shared_down, preferred_element_type=jnp.float32)  6.46 us
  transfers between devices with their start and end apart: 5, of which 5 were waited for; matrix products, arithmetic and copies ran while one was open for 6% of the time, Pallas kernels for 0%

profile of v1, /device:TPU:0, one launch (start us, length us, event | category | flops | bytes accessed | tf_op | source)
XLA Modules:
  0.0 315.6 jit_solution(17590369145521392428)
XLA Ops:
  6.6 4.0 %collective-permute-start = (bf16[128,5120]{1,0:T(8,128)(2,1)}, bf16[128,5120]{1,0:T(8,128)(2,1)S(1)}, u32[]{:S(2)}, u32[]{:S(2)}) collective-permute-start(bf16[128,5120]{1,0:T(8,128)(2,1)} %param.11), channel_id=1, source_target_pairs={{0,24},{8,0},{16,8},{24,16},{1,25},{9,1},{17,9},{25,17},{2,26},{10... | collective-permute-start | bytes 3932168 | tf_op jit(solution)/shard_map/ppermute | solution.py:17
  10.6 28.4 %collective-permute-done = bf16[128,5120]{1,0:T(8,128)(2,1)S(1)} collective-permute-done((bf16[128,5120]{1,0:T(8,128)(2,1)}, bf16[128,5120]{1,0:T(8,128)(2,1)S(1)}, u32[]{:S(2)}, u32[]{:S(2)}) %collective-permute-start) | collective-permute-done | bytes 1310752 | tf_op jit(solution)/shard_map/ppermute | solution.py:17
  38.9 3.5 %pad_maximum_fusion = bf16[256,5120]{1,0:T(8,128)(2,1)} fusion(bf16[128,5120]{1,0:T(8,128)(2,1)S(1)} %collective-permute-done, bf16[128,5120]{1,0:T(8,128)(2,1)} %param.11), kind=kLoop, calls=%fused_computation.10 | loop fusion | flops 5242880 | bytes 5242880 | tf_op jit(solution)/shard_map/concatenate | solution.py:22
  42.4 1.4 collective-permute-start.1
  43.9 0.3 reduce-window.24
  44.2 0.1 slice.16
  44.3 0.3 reduce-window.16
  44.6 0.1 slice.14
  44.7 0.7 constant_dynamic-slice_fusion.1
  46.7 0.1 slice_reduce_fusion
  46.9 0.1 broadcast_compare_fusion.1
  47.0 1.5 constant_dynamic-update-slice_fusion.5
  48.5 0.1 constant_dynamic-update-slice_fusion.4
  48.6 51.9 %collective-permute-done.1 = bf16[256,5120]{1,0:T(8,128)(2,1)} collective-permute-done((bf16[256,5120]{1,0:T(8,128)(2,1)}, bf16[256,5120]{1,0:T(8,128)(2,1)}, u32[]{:S(2)}, u32[]{:S(2)}) %collective-permute-start.1) | collective-permute-done | bytes 2621472 | tf_op jit(solution)/shard_map/ppermute | solution.py:17
  100.5 2.1 constant_dynamic-update-slice_fusion.3
  102.5 0.1 constant_dynamic-update-slice_fusion.2
  102.6 0.1 constant_dynamic-update-slice_fusion.1
  102.8 2.1 constant_dynamic-update-slice_fusion
  104.8 4.0 %copy-done.4 = bf16[1024,5120]{1,0:T(8,128)(2,1)} copy-done((bf16[1024,5120]{1,0:T(8,128)(2,1)}, bf16[1024,5120]{1,0:T(8,128)(2,1)S(1)}, u32[]{:S(2)}) %copy-start.4) | copy-done | bytes 10485784
  108.8 1.0 convolution_convert_fusion
  109.8 0.3 fusion.20
  110.2 2.0 fusion.4
  112.2 11.9 %fusion = f32[64,5120]{1,0:T(8,128)} fusion(bf16[1,1024,5120]{2,1,0:T(8,128)(2,1)} %param.18, bf16[1,5120,1024]{2,1,0:T(8,128)(2,1)} %param.17, bf16[64,5120]{1,0:T(8,128)(2,1)S(1)} %convolution_convert_fusion, f32[64]{0:T(128)S(1)} %fusion.20, f32[64,1024]{1,0:T(8,128)S(1)} %fusion.4), kind=kOutput, calls=%fused_computation.1 | convolution fusion | flops 1343553536 | bytes 23200000 | tf_op jit(solution)/shard_map/dot_general | solution.py:76
  124.2 5.3 %fusion.10 = f32[512,1024]{1,0:T(8,128)} fusion(bf16[1280,1024]{1,0:T(8,128)(2,1)} %param.20, bf16[1024,5120]{1,0:T(8,128)(2,1)} %copy-done.4, s32[]{:T(128)S(6)} %select_n.48, s32[]{:T(128)S(6)} %select_n.50), kind=kOutput, calls=%fused_computation.14 | convolution fusion | flops 1342177280 | bytes 6029320 | tf_op jit(solution)/shard_map/dot_general | solution.py:81
  129.4 4.3 %fusion.12 = f32[512,1024]{1,0:T(8,128)} fusion(bf16[1280,1024]{1,0:T(8,128)(2,1)S(1)} %copy-done.8, bf16[1024,5120]{1,0:T(8,128)(2,1)} %copy-done.4, s32[]{:T(128)S(6)} %select_n.48, s32[]{:T(128)S(6)} %select_n.50), kind=kOutput, calls=%fused_computation.16 | convolution fusion | flops 1342177280 | bytes 6029320 | tf_op jit(solution)/shard_map/dot_general | solution.py:80
  133.8 0.2 reduce-scatter.5.cloned.1.call-start
  134.0 21.8 %reduce-scatter.3.cloned.1.call-done = f32[64,1280]{1,0:T(8,128)} async-done(((f32[64,5120]{1,0:T(8,128)}), f32[64,1280]{1,0:T(8,128)}) %reduce-scatter.3.cloned.1.call-update) | async-done | bytes 327696 | tf_op jit(solution)/shard_map/reduce_scatter | solution.py:85
  155.8 5.0 %gather_fusion = f32[512,1280]{1,0:T(8,128)} fusion(f32[64,1280]{1,0:T(8,128)} %reduce-scatter.3.cloned.1.call-done, s32[1024]{0:T(1024)S(1)} %pad_clamp_fusion), kind=kCustom, calls=%fused_computation | custom fusion | bytes 5244928 | tf_op jit(solution)/shard_map/jit(_take)/gather | solution.py:49
  160.8 102.1 %all-reduce.3.cloned.1.call-done = (f32[512,1024]{1,0:T(8,128)}, f32[512,1024]{1,0:T(8,128)}) async-done(((f32[512,1024]{1,0:T(8,128)}, f32[512,1024]{1,0:T(8,128)}), (f32[512,1024]{1,0:T(8,128)}, f32[512,1024]{1,0:T(8,128)})) %all-reduce.3.cloned.1.call-update) | async-done | bytes 4194320 | tf_op jit(solution)/shard_map/psum | solution.py:82
  262.9 6.5 %convolution_add_fusion = f32[512,1280]{1,0:T(8,128)} fusion(bf16[1024,1280]{1,0:T(8,128)(2,1)S(1)} %copy-done, f32[512,1280]{1,0:T(8,128)} %gather_fusion, pred[512]{0:T(512)(128)(4,1)S(1)} %broadcast_compare_fusion, pred[512]{0:T(512)(128)(4,1)S(1)} %get-tuple-element.7, f32[512,1024]{1,0:T(8,128)} %get-tuple-element.5, f32[512,1024]{1,0:T(8,128)} %get-tuple-element.6), kind=kOutput, calls=%fused_computation.9 | convolution fusion | flops 1347289088 | bytes 12059648 | tf_op jit(solution)/shard_map/dot_general | solution.py:84
  269.4 38.0 %reduce-scatter.5.cloned.1.call-done = f32[64,1280]{1,0:T(8,128)} async-done(((f32[512,1280]{1,0:T(8,128)}), f32[64,1280]{1,0:T(8,128)}) %reduce-scatter.5.cloned.1.call-update) | async-done | bytes 327696 | tf_op jit(solution)/shard_map/reduce_scatter | solution.py:87
  307.4 1.7 convert_element_type.32
  (38 shorter events, 0.3 us)
Async XLA Ops:
  6.5 256.4 %copy-start = (bf16[1024,1280]{1,0:T(8,128)(2,1)S(1)}, bf16[1024,1280]{1,0:T(8,128)(2,1)}, u32[]{:S(2)}) copy-start(bf16[1024,1280]{1,0:T(8,128)(2,1)} %param.21) | copy-start | bytes 7864324
  6.5 37.3 %copy-start.5 = (s32[512]{0:T(512)S(1)}, s32[512]{0:T(512)}, u32[]{:S(2)}) copy-start(s32[512]{0:T(512)} %param.13) | copy-start | bytes 6148
  6.5 37.3 %copy-start.6 = (s32[512]{0:T(512)S(1)}, s32[512]{0:T(512)}, u32[]{:S(2)}) copy-start(s32[512]{0:T(512)} %param.12) | copy-start | bytes 6148
  6.5 38.2 %copy-start.7 = (s32[2,8]{1,0:T(2,128)S(1)}, s32[2,8]{1,0:T(2,128)}, u32[]{:S(2)}) copy-start(s32[2,8]{1,0:T(2,128)} %param.14) | copy-start | bytes 196
  6.5 149.2 %reduce-scatter.3.cloned.1.call-start = ((), (), s32[]{:S(2)}) async-start(), calls=%async_computation.2 | async-start | bytes 1638400 | tf_op jit(solution)/shard_map/reduce_scatter | solution.py:85
  6.6 32.3 %collective-permute-start = (bf16[128,5120]{1,0:T(8,128)(2,1)}, bf16[128,5120]{1,0:T(8,128)(2,1)S(1)}, u32[]{:S(2)}, u32[]{:S(2)}) collective-permute-start(bf16[128,5120]{1,0:T(8,128)(2,1)} %param.11), channel_id=1, source_target_pairs={{0,24},{8,0},{16,8},{24,16},{1,25},{9,1},{17,9},{25,17},{2,26},{10... | collective-permute-start | bytes 3932168 | tf_op jit(solution)/shard_map/ppermute | solution.py:17
  38.9 3.5 %copy-start.2 = (bf16[128,5120]{1,0:T(8,128)(2,1)}, bf16[128,5120]{1,0:T(8,128)(2,1)S(1)}, u32[]{:S(2)}) copy-start(bf16[128,5120]{1,0:T(8,128)(2,1)S(1)} %collective-permute-done) | copy-start | bytes 3932164
  42.4 58.1 %collective-permute-start.1 = (bf16[256,5120]{1,0:T(8,128)(2,1)}, bf16[256,5120]{1,0:T(8,128)(2,1)}, u32[]{:S(2)}, u32[]{:S(2)}) collective-permute-start(bf16[256,5120]{1,0:T(8,128)(2,1)} %pad_maximum_fusion), channel_id=1, source_target_pairs={{0,16},{8,24},{16,0},{24,8},{1,17},{9,25},{17,1},{25,9},{2,18},{10... | collective-permute-start | bytes 7864328 | tf_op jit(solution)/shard_map/ppermute | solution.py:17
  46.7 1.8 copy-start.3
  48.6 53.9 %copy-start.1 = (bf16[128,5120]{1,0:T(8,128)(2,1)S(1)}, bf16[128,5120]{1,0:T(8,128)(2,1)}, u32[]{:S(2)}) copy-start(bf16[128,5120]{1,0:T(8,128)(2,1)} %param.11) | copy-start | bytes 3932164
  100.5 9.6 %slice-start = ((s8[10485760]{0:T(1024)(128)(4,1)}), s8[4194304]{0:T(1024)(128)(4,1)S(1)}, s32[]{:S(2)}) async-start(s8[10485760]{0:T(1024)(128)(4,1)} %bitcast.56), calls=%async_computation.5 | async-start | bytes 8388608
  102.5 7.6 %slice-start.1 = ((s8[10485760]{0:T(1024)(128)(4,1)}), s8[4194304]{0:T(1024)(128)(4,1)S(1)}, s32[]{:S(2)}) async-start(s8[10485760]{0:T(1024)(128)(4,1)} %bitcast.56), calls=%async_computation.6 | async-start | bytes 8388608
  102.7 7.4 %slice-start.2 = ((s8[10485760]{0:T(1024)(128)(4,1)}), s8[2097152]{0:T(1024)(128)(4,1)S(1)}, s32[]{:S(2)}) async-start(s8[10485760]{0:T(1024)(128)(4,1)} %bitcast.56), calls=%async_computation.7 | async-start | bytes 4194304
  104.8 4.0 %copy-start.4 = (bf16[1024,5120]{1,0:T(8,128)(2,1)}, bf16[1024,5120]{1,0:T(8,128)(2,1)S(1)}, u32[]{:S(2)}) copy-start(bf16[1024,5120]{1,0:T(8,128)(2,1)S(1)} %constant_dynamic-update-slice_fusion) | copy-start | bytes 31457284
  108.8 1.0 copy-start.9
  124.1 138.8 %all-reduce.3.cloned.1.call-start = ((), (), s32[]{:S(2)}) async-start(), calls=%async_computation.4 | async-start | bytes 8388608 | tf_op jit(solution)/shard_map/psum | solution.py:82
  124.2 5.3 %copy-start.8 = (bf16[1280,1024]{1,0:T(8,128)(2,1)S(1)}, bf16[1280,1024]{1,0:T(8,128)(2,1)}, u32[]{:S(2)}) copy-start(bf16[1280,1024]{1,0:T(8,128)(2,1)} %param.19) | copy-start | bytes 7864324
  133.8 173.6 %reduce-scatter.5.cloned.1.call-start = ((), (), s32[]{:S(2)}) async-start(), calls=%async_computation.3 | async-start | bytes 2949120 | tf_op jit(solution)/shard_map/reduce_scatter | solution.py:87
Sparse Core Ops, SparseCore 0:
  124.2 31.5 reduce-scatter.2
  159.3 103.5 all-reduce.2
  269.5 37.8 reduce-scatter.4
